TPU v7x, 512 devices: a whole 4x4x16 slice. The times are simulated.
512 devices in a mesh: frames: 64 (over z, y), strips: 8 (over x, core).
Axes of the slice: x: 4, y: 4, z: 16, core: 2. Of those that a mesh axis runs over, the one named last changes fastest.
Arguments:
- raw_frames: bfloat16 [4096, 512, 512], P('frames', 'strips'), may hold values from -24 to 24
- dark_frame: float32 [512, 512], P('strips'), may hold values from -6 to 6
- dead_mask: int32 [512, 512], P('strips'), may hold values 0 or 1
- frame_group: int32 [4096], P('frames'), may hold values from 0 to 7
- prior_sigma: float32 [128], replicated, may hold values from 0.2 to 0.5
- start_rotation: float32 [128, 128], replicated, as said below
- basis: bfloat16 [262144, 128], P(('strips', 'frames')), may hold values from -0.01171875 to 0.01171875
Outputs:
- new_basis: bfloat16 [262144, 128], P(('strips', 'frames'))
- new_coeffs: float32 [4096, 128], P('frames')
- new_sigma: float32 [128], replicated
Inputs may be any that keep to these rules, and one draw needn't show every extreme that they name: start_rotation is nonsingular.
All inputs are finite; a program needn't handle non-finite values. No bound on the sum of `dead_mask` on one device may be relied on, other than what follows from the above.
Results may differ from a plain program's by a relative error of at most 0.0071.
Values may be sent and summed in bfloat16 or wider, within the bound.
A program may use at most 64 MiB of HBM per device.

v0:
```python
import jax
import jax.numpy as jnp
from jax import lax
from jax.sharding import PartitionSpec as P

GROUPS = 8
ITERS = 4


BLUR_TAPS = (1.0 / 64, 6.0 / 64, 15.0 / 64, 20.0 / 64, 15.0 / 64, 6.0 / 64, 1.0 / 64)
DECAY_RATE = 0.7


def extended(shard, sides, width):
    for axis, dim in sides:
        size, length = (lax.axis_size(axis), shard.shape[dim])
        up = [(i, (i + 1) % size) for i in range(size - 1)]
        down = [(j, i) for i, j in up]
        last = lax.slice_in_dim(shard, length - width, length, axis=dim)
        first = lax.slice_in_dim(shard, 0, width, axis=dim)
        before = lax.ppermute(last, axis, up)
        after = lax.ppermute(first, axis, down)
        shard = jnp.concatenate([before, shard, after], axis=dim)
    return shard


def orthonormalize(product):
    normal = jnp.dot(product.T, product, precision=lax.Precision.HIGHEST)
    factor = jnp.linalg.cholesky(normal)
    return lax.linalg.triangular_solve(
        factor, product, left_side=False, lower=True, transpose_a=True
    )


def body(raw_frames, dark_frame, dead_mask, frame_group, prior_sigma, start_rotation, basis):
    frame_count, strip_rows, columns = raw_frames.shape
    corrected = (
        (raw_frames.astype(jnp.float32) - dark_frame) * (1 - dead_mask).astype(jnp.float32)
    ).astype(jnp.bfloat16)
    position = jnp.arange(columns)
    offsets = position[None, :] - position[:, None]
    banded = jnp.zeros((columns, columns), jnp.float32)
    for shift_by in range(-3, 4):
        banded = banded + jnp.where(offsets == shift_by, BLUR_TAPS[shift_by + 3], 0.0)
    banded = banded.astype(jnp.bfloat16)
    column_blur = jnp.dot(
        corrected.reshape(frame_count * strip_rows, columns),
        banded,
        preferred_element_type=jnp.float32,
    )
    column_blur = column_blur.reshape(frame_count, strip_rows, columns)
    padded = extended(column_blur, (("strips", 1),), 3)
    row_blur = BLUR_TAPS[0] * padded[:, 0:strip_rows, :]
    for offset in range(1, 7):
        row_blur = row_blur + BLUR_TAPS[offset] * padded[:, offset : offset + strip_rows, :]
    frame_weight = jnp.power(
        jnp.float32(DECAY_RATE), (GROUPS - 1 - frame_group).astype(jnp.float32)
    )
    weighted = (
        (frame_weight[:, None, None] * row_blur)
        .astype(jnp.bfloat16)
        .reshape(frame_count, strip_rows * columns)
    )
    partial_value = jnp.dot(
        weighted,
        lax.all_gather(basis, "frames", axis=0, tiled=True),
        preferred_element_type=jnp.float32,
    )
    coeffs = lax.psum(partial_value, "strips")
    total_frames = frame_count * lax.axis_size("frames")
    local_gram = jnp.dot(coeffs.T, coeffs, precision=lax.Precision.HIGHEST)
    summed_gram = lax.psum(local_gram, "frames")
    gram = jnp.diag(prior_sigma * prior_sigma) + summed_gram / total_frames
    rotation = start_rotation
    for step in range(ITERS):
        rotation = orthonormalize(jnp.dot(gram, rotation, precision=lax.Precision.HIGHEST))
    new_coeffs = jnp.dot(coeffs, rotation, precision=lax.Precision.HIGHEST)
    new_basis = jnp.dot(
        basis.astype(jnp.float32), rotation, precision=lax.Precision.HIGHEST
    ).astype(jnp.bfloat16)
    curved = jnp.dot(gram, rotation, precision=lax.Precision.HIGHEST)
    new_sigma = jnp.sqrt(jnp.sum(rotation * curved, axis=0))
    return (new_basis, new_coeffs, new_sigma)


def solution(mesh):
    placed = (
        P("frames", "strips", None),
        P("strips", None),
        P("strips", None),
        P("frames"),
        P(),
        P(),
        P(("strips", "frames"), None),
    )
    return jax.shard_map(
        body,
        mesh=mesh,
        in_specs=placed,
        out_specs=(P(("strips", "frames"), None), P("frames", None), P()),
        check_vma=False,
    )
```

profile of v0, /device:TPU:1, one launch (start us, length us, event | category | flops | bytes accessed | tf_op | source)
XLA Modules:
  0.0 553.4 jit_solution(2204300600447689643)
XLA Ops:
  7.2 0.7 all-gather.2.cloned.1.call-update
  8.0 0.9 subtract_convert_fusion
  8.9 4.7 fusion.18
  13.9 4.5 collective-permute-start
  18.4 5.6 %collective-permute-start.1 = (f32[64,3,512]{2,1,0:T(4,128)S(1)}, f32[64,3,512]{2,1,0:T(4,128)S(1)}, u32[]{:S(2)}, u32[]{:S(2)}) collective-permute-start(f32[64,3,512]{2,1,0:T(4,128)S(1)} %get-tuple-element.9), channel_id=1, source_target_pairs={{1,0},{2,1},{3,2},{4,3},{5,4},{6,5},{7,6},{9,8},{10,9},{11,10},{12... | collective-permute-start | bytes 1179656 | tf_op jit(solution)/shard_map/ppermute | solution.py:22
  24.5 4.4 collective-permute-done.1
  28.9 8.9 %fusion.5 = bf16[64,64,512]{2,1,0:T(8,128)(2,1)S(1)} fusion(f32[64,64,512]{2,1,0:T(8,128)S(1)} %fusion.18, f32[64,3,512]{2,1,0:T(4,128)S(1)} %collective-permute-done.1, f32[64,3,512]{2,1,0:T(4,128)S(1)} %collective-permute-done, f32[64]{0:T(128)S(1)} %convert_power_fusion), kind=kLoop, calls=%fused_computation.13 | loop fusion | flops 44040192 | bytes 13369600 | tf_op jit(solution)/shard_map/convert_element_type | solution.py:61
  37.8 4.5 copy.15
  42.3 123.2 %all-gather.2.cloned.1.call-done = bf16[32768,128]{1,0:T(8,128)(2,1)} async-done(((bf16[512,128]{1,0:T(8,128)(2,1)}), bf16[32768,128]{1,0:T(8,128)(2,1)}) %all-gather.2.cloned.1.call-update) | async-done | bytes 8388624 | tf_op jit(solution)/shard_map/all_gather | solution.py:66
  165.5 6.3 %fusion.86 = f32[64,128]{1,0:T(8,128)S(1)} fusion(bf16[64,32768]{1,0:T(8,128)(2,1)} %bitcast.76, bf16[32768,128]{1,0:T(8,128)(2,1)} %all-gather.2.cloned.1.call-done), kind=kOutput, calls=%fused_computation.116 | convolution fusion | flops 536870912 | bytes 12615680 | tf_op jit(solution)/shard_map/dot_general | solution.py:64
  171.8 28.5 %psum.14 = f32[64,128]{1,0:T(8,128)S(1)} all-reduce(f32[64,128]{1,0:T(8,128)S(1)} %fusion.86), channel_id=1, replica_groups=mesh['frames'=64,'strips'=8] {'strips'}, use_global_device_ids=true, to_apply=%region_0.1 | all-reduce | flops 8192 | bytes 65536 | tf_op jit(solution)/shard_map/psum | solution.py:69
  200.3 0.9 fusion.87
  201.3 242.7 %all-reduce.2.cloned.1.call-done = f32[128,128]{1,0:T(8,128)} async-done(((f32[128,128]{1,0:T(8,128)}), f32[128,128]{1,0:T(8,128)}) %all-reduce.2.cloned.1.call-update) | async-done | bytes 65552 | tf_op jit(solution)/shard_map/psum | solution.py:72
  444.0 1.1 fusion.83
  445.5 11.7 %cholesky.74 = f32[128,128]{1,0:T(8,128)S(1)} custom-call(f32[128,128]{1,0:T(8,128)S(1)} %fusion.55), custom_call_target="Cholesky" | custom-call | tf_op jit(solution)/shard_map/jit(cholesky)/cholesky | solution.py:29
  457.9 0.7 fusion.44
  458.5 9.8 %custom-call.8 = f32[1,128,128]{1,2,0:T(8,128)S(1)} custom-call(f32[1,128,128]{2,1,0:T(8,128)S(1)} %fusion.44), custom_call_target="InvertDiagBlocksLowerTriangular" | custom-call | tf_op jit(solution)/shard_map/triangular_solve/custom-call.0 | solution.py:30
  468.7 1.1 fusion.81
  470.2 11.7 %cholesky.85 = f32[128,128]{1,0:T(8,128)S(1)} custom-call(f32[128,128]{1,0:T(8,128)S(1)} %fusion.53), custom_call_target="Cholesky" | custom-call | tf_op jit(solution)/shard_map/jit(cholesky)/cholesky | solution.py:29
  482.6 0.7 fusion.45
  483.3 10.0 %custom-call.9 = f32[1,128,128]{1,2,0:T(8,128)S(1)} custom-call(f32[1,128,128]{2,1,0:T(8,128)S(1)} %fusion.45), custom_call_target="InvertDiagBlocksLowerTriangular" | custom-call | tf_op jit(solution)/shard_map/triangular_solve/custom-call.0 | solution.py:30
  493.5 1.1 fusion.79
  495.1 11.7 %cholesky.96 = f32[128,128]{1,0:T(8,128)S(1)} custom-call(f32[128,128]{1,0:T(8,128)S(1)} %fusion.51), custom_call_target="Cholesky" | custom-call | tf_op jit(solution)/shard_map/jit(cholesky)/cholesky | solution.py:29
  507.5 0.7 fusion.46
  508.2 9.8 %custom-call.10 = f32[1,128,128]{1,2,0:T(8,128)S(1)} custom-call(f32[1,128,128]{2,1,0:T(8,128)S(1)} %fusion.46), custom_call_target="InvertDiagBlocksLowerTriangular" | custom-call | tf_op jit(solution)/shard_map/triangular_solve/custom-call.0 | solution.py:30
  518.3 1.1 fusion.77
  519.8 11.7 %cholesky.107 = f32[128,128]{1,0:T(8,128)S(1)} custom-call(f32[128,128]{1,0:T(8,128)S(1)} %fusion.49), custom_call_target="Cholesky" | custom-call | tf_op jit(solution)/shard_map/jit(cholesky)/cholesky | solution.py:29
  532.2 0.7 fusion.47
  532.9 10.0 %custom-call.11 = f32[1,128,128]{1,2,0:T(8,128)S(1)} custom-call(f32[1,128,128]{2,1,0:T(8,128)S(1)} %fusion.47), custom_call_target="InvertDiagBlocksLowerTriangular" | custom-call | tf_op jit(solution)/shard_map/triangular_solve/custom-call.0 | solution.py:30
  543.1 0.8 fusion.92
  544.2 1.1 fusion.22
  545.8 0.8 copy.14
  (41 shorter events, 7.0 us)
Async XLA Ops:
  7.2 436.8 %copy-start = (f32[128,128]{1,0:T(8,128)S(1)}, f32[128,128]{1,0:T(8,128)}, u32[]{:S(2)}) copy-start(f32[128,128]{1,0:T(8,128)} %param.15) | copy-start | bytes 196612
  7.2 158.4 %all-gather.2.cloned.1.call-start = ((), (), s32[]{:S(2)}) async-start(), calls=%async_computation | async-start | bytes 8519680 | tf_op jit(solution)/shard_map/all_gather | solution.py:66
  7.9 436.1 %all-reduce.2.cloned.1.call-start = ((), (), s32[]{:S(2)}) async-start(), calls=%async_computation.1 | async-start | bytes 131072 | tf_op jit(solution)/shard_map/psum | solution.py:72
  8.9 15.1 %copy-start.2 = (s32[64]{0:T(128)S(1)}, s32[64]{0:T(128)}, u32[]{:S(2)}) copy-start(s32[64]{0:T(128)} %param.13) | copy-start | bytes 772
  13.9 10.6 %collective-permute-start = (f32[64,3,512]{2,1,0:T(4,128)S(1)}, f32[64,3,512]{2,1,0:T(4,128)S(1)}, u32[]{:S(2)}, u32[]{:S(2)}) collective-permute-start(f32[64,3,512]{2,1,0:T(4,128)S(1)} %get-tuple-element.8), channel_id=1, source_target_pairs={{0,1},{1,2},{2,3},{3,4},{4,5},{5,6},{6,7},{8,9},{9,10},{10,11},{11... | collective-permute-start | bytes 1179656 | tf_op jit(solution)/shard_map/ppermute | solution.py:21
  18.4 10.5 %collective-permute-start.1 = (f32[64,3,512]{2,1,0:T(4,128)S(1)}, f32[64,3,512]{2,1,0:T(4,128)S(1)}, u32[]{:S(2)}, u32[]{:S(2)}) collective-permute-start(f32[64,3,512]{2,1,0:T(4,128)S(1)} %get-tuple-element.9), channel_id=1, source_target_pairs={{1,0},{2,1},{3,2},{4,3},{5,4},{6,5},{7,6},{9,8},{10,9},{11,10},{12... | collective-permute-start | bytes 1179656 | tf_op jit(solution)/shard_map/ppermute | solution.py:22
  165.5 35.7 %copy-start.3 = (f32[128]{0:T(128)S(1)}, f32[128]{0:T(128)}, u32[]{:S(2)}) copy-start(f32[128]{0:T(128)} %param.14) | copy-start | bytes 1540
  165.5 378.3 %copy-start.1 = (bf16[512,128]{1,0:T(8,128)(2,1)S(1)}, bf16[512,128]{1,0:T(8,128)(2,1)}, u32[]{:S(2)}) copy-start(bf16[512,128]{1,0:T(8,128)(2,1)} %param.16) | copy-start | bytes 393220
Sparse Core Ops, SparseCore 0:
  11.0 154.5 all-gather.1
  201.4 242.5 all-reduce.1
where the time goes:
time: 563 us; the launch traced here: 553 us
  waiting for transfers between devices  371 us (66%)
  other arithmetic  102 us (18%)
  blocking collectives  28.5 us (5%)
  matrix products  20.9 us (4%)
  between operations  14.3 us (3%)
  starting transfers between devices  10.2 us (2%)
  local copies, waits for them, and re-layouts  6.45 us (1%)
    psum x1, waiting for transfers between devices, body(): summed_gram = lax.psum(local_gram, 'frames')  243 us
    all_gather x1, waiting for transfers between devices, body(): lax.all_gather(basis, 'frames', axis=0, tiled=True)  123 us
    another operation x12, other arithmetic, orthonormalize(): factor = jnp.linalg.cholesky(normal)  49.6 us
    another operation x8, other arithmetic, orthonormalize(): lax.linalg.triangular_solve(factor, product, left_side=False, lower=True,...  42.2 us
    psum x1, blocking collectives, body(): coeffs = lax.psum(partial_value, 'strips')  28.5 us
  transfers between devices with their start and end apart: 4, of which 4 were waited for; matrix products, arithmetic and copies ran while one was open for 3% of the time, Pallas kernels for 0%

commit v1 on v0

--- a/solution.py
+++ b/solution.py
@@ -1,14 +1,21 @@
+import functools
+
 import jax
 import jax.numpy as jnp
 from jax import lax
+from jax.experimental import pallas as pl
+from jax.experimental.pallas import tpu as pltpu
 from jax.sharding import PartitionSpec as P
 
 GROUPS = 8
 ITERS = 4
-
+K = 128
+Y = 4
 
 BLUR_TAPS = (1.0 / 64, 6.0 / 64, 15.0 / 64, 20.0 / 64, 15.0 / 64, 6.0 / 64, 1.0 / 64)
 DECAY_RATE = 0.7
+MESH = pl.DeviceIdType.MESH
+HIGHEST = lax.Precision.HIGHEST
 
 
 def extended(shard, sides, width):
@@ -24,12 +31,184 @@
     return shard
 
 
-def orthonormalize(product):
-    normal = jnp.dot(product.T, product, precision=lax.Precision.HIGHEST)
-    factor = jnp.linalg.cholesky(normal)
-    return lax.linalg.triangular_solve(
-        factor, product, left_side=False, lower=True, transpose_a=True
-    )
+def reduce_kernel(Z, S, part_ref, coeffs_ref, gram_ref,
+                  parts, local, ybuf, zbuf, full,
+                  s1, r1, s2, r2, s3, r3, s4, r4):
+    f, s = lax.axis_index("frames"), lax.axis_index("strips")
+    z, y = f // Y, f % Y
+    NB = 2 * S
+    rows = K // NB
+    strip_peers = [(f, (s + d) % S) for d in range(1, S)]
+    y_peers = [(z * Y + (y + d) % Y, s) for d in range(1, Y)]
+    z_peers = [(((z + d) % Z) * Y + y, s) for d in range(1, Z)]
+    f_cross = z * Y + (y + 2) % Y
+    cross_peers = [(f_cross, (s + d) % S) for d in range(1, S)]
+    barrier = pltpu.get_barrier_semaphore()
+    everyone = strip_peers + y_peers + z_peers + cross_peers
+    for peer in everyone:
+        pl.semaphore_signal(barrier, inc=1, device_id=peer, device_id_type=MESH)
+    pl.semaphore_wait(barrier, len(everyone))
+
+    def send(src, dst, ssem, rsem, peer):
+        copy = pltpu.make_async_remote_copy(
+            src_ref=src, dst_ref=dst, send_sem=ssem, recv_sem=rsem,
+            device_id=peer, device_id_type=MESH)
+        copy.start()
+        return copy
+
+    def arrived(ref, sem):
+        pltpu.make_async_copy(ref, ref, sem).wait()
+
+    sent = [send(part_ref, parts.at[s], s1.at[d], r1.at[s], peer)
+            for d, peer in enumerate(strip_peers)]
+    parts[s] = part_ref[...]
+    for d in range(1, S):
+        other = (s + d) % S
+        arrived(parts.at[other], r1.at[other])
+    coeffs = parts[0]
+    for i in range(1, S):
+        coeffs = coeffs + parts[i]
+    coeffs_ref[...] = coeffs
+    gram = lax.dot_general(coeffs, coeffs, (((0,), (0,)), ((), ())), precision=HIGHEST,
+                           preferred_element_type=jnp.float32)
+    local[...] = gram.reshape(NB, rows, K)
+
+    for d, peer in enumerate(y_peers):
+        block = 2 * s + ((y + d + 1) % Y) // 2
+        sent.append(send(local.at[block], ybuf.at[y], s2.at[d], r2.at[y], peer))
+    mine = 2 * s + y // 2
+    ybuf[y] = local[mine]
+    for d in range(1, Y):
+        other = (y + d) % Y
+        arrived(ybuf.at[other], r2.at[other])
+    zbuf[z] = (ybuf[0] + ybuf[1]) + (ybuf[2] + ybuf[3])
+
+    for d, peer in enumerate(z_peers):
+        sent.append(send(zbuf.at[z], zbuf.at[z], s3.at[d], r3.at[z], peer))
+    for d in range(1, Z):
+        other = (z + d) % Z
+        arrived(zbuf.at[other], r3.at[other])
+    total = zbuf[0]
+    for i in range(1, Z):
+        total = total + zbuf[i]
+    full[mine] = total
+
+    fourth = strip_peers + [(f_cross, (s + d) % S) for d in range(S)]
+    for d, peer in enumerate(fourth):
+        sent.append(send(full.at[mine], full.at[mine], s4.at[d], r4.at[mine], peer))
+    for d in range(1, NB):
+        other = (mine + d) % NB
+        arrived(full.at[other], r4.at[other])
+    gram_ref[...] = full[...].reshape(K, K)
+    for copy in sent:
+        copy.wait_send()
+
+
+def reduced(part, Z, S):
+    frames = part.shape[0]
+    rows = K // (2 * S)
+    dma = pltpu.SemaphoreType.DMA
+    vmem = pl.BlockSpec(memory_space=pltpu.VMEM)
+    return pl.pallas_call(
+        functools.partial(reduce_kernel, Z, S),
+        out_shape=(jax.ShapeDtypeStruct((frames, K), jnp.float32),
+                   jax.ShapeDtypeStruct((K, K), jnp.float32)),
+        in_specs=[vmem],
+        out_specs=(vmem, vmem),
+        scratch_shapes=[
+            pltpu.VMEM((S, frames, K), jnp.float32),
+            pltpu.VMEM((2 * S, rows, K), jnp.float32),
+            pltpu.VMEM((Y, rows, K), jnp.float32),
+            pltpu.VMEM((Z, rows, K), jnp.float32),
+            pltpu.VMEM((2 * S, rows, K), jnp.float32),
+            dma((S,)), dma((S,)), dma((Y,)), dma((Y,)),
+            dma((Z,)), dma((Z,)), dma((2 * S,)), dma((2 * S,)),
+        ],
+        compiler_params=pltpu.CompilerParams(collective_id=0, has_side_effects=True),
+    )(part)
+
+
+def pieces(x):
+    high = x.astype(jnp.bfloat16).astype(jnp.float32)
+    rest = x - high
+    middle = rest.astype(jnp.bfloat16).astype(jnp.float32)
+    return high, middle, rest - middle
+
+
+def rotate_kernel(total_frames, gram_ref, prior_ref, start_ref, coeffs_ref, basis_ref,
+                  basis_out, coeffs_out, sigma_out, G, RT, M):
+    b = 8
+    row = lax.broadcasted_iota(jnp.int32, (K, K), 0)
+    column = lax.broadcasted_iota(jnp.int32, (K, K), 1)
+    prior = prior_ref[...]
+    G[...] = jnp.where(row == column, prior * prior, 0.0) + gram_ref[...] * (1.0 / total_frames)
+    RT[...] = start_ref[...].T
+    sub = lax.broadcasted_iota(jnp.int32, (b, K), 0)
+
+    def step(_, carry):
+        product_t = jnp.dot(RT[...], G[...], precision=HIGHEST,
+                            preferred_element_type=jnp.float32)
+        M[:, :K] = lax.dot_general(product_t, product_t, (((1,), (1,)), ((), ())),
+                                   precision=HIGHEST, preferred_element_type=jnp.float32)
+        M[:, K:] = product_t
+        for j in range(K // b):
+            at = j * b
+            left, right = M[at:at + b, :K], M[at:at + b, K:]
+            cols = [jnp.broadcast_to(left[:, at + i:at + i + 1], (b, K)) for i in range(b)]
+            scale = jnp.zeros((b, K), jnp.float32)
+            for i in range(b):
+                pivot = jnp.broadcast_to(cols[i][i:i + 1], (b, K))
+                scale = jnp.where(sub == i, lax.rsqrt(pivot), scale)
+                if i < b - 1:
+                    factor = jnp.where(sub > i, cols[i] / pivot, 0.0)
+                    for c in range(i + 1, b):
+                        cols[c] = cols[c] - factor * cols[c][i:i + 1]
+                    left = left - factor * left[i:i + 1]
+                    right = right - factor * right[i:i + 1]
+            left, right = left * scale, right * scale
+            RT[at:at + b, :] = right
+            if at + b < K:
+                h, m, l = pieces(left)
+                hr, mr, lr = pieces(right)
+                lhs = jnp.concatenate([h, h, m, m, h, l], axis=0).astype(jnp.bfloat16)
+                rhs_l = jnp.concatenate([h, m, h, m, l, h], axis=0)
+                rhs_r = jnp.concatenate([hr, mr, hr, mr, lr, hr], axis=0)
+                rhs = jnp.concatenate([rhs_l, rhs_r], axis=1).astype(jnp.bfloat16)
+                update = lax.dot_general(lhs, rhs, (((0,), (0,)), ((), ())),
+                                         preferred_element_type=jnp.float32)
+                M[at + b:, :] = M[at + b:, :] - update[at + b:, :]
+        return carry
+
+    lax.fori_loop(0, ITERS, step, 0)
+    rotation_t = RT[...]
+    across = (((1,), (1,)), ((), ()))
+    coeffs_out[...] = lax.dot_general(coeffs_ref[...], rotation_t, across, precision=HIGHEST,
+                                      preferred_element_type=jnp.float32)
+    basis = basis_ref[...]
+    high, middle, low = (p.astype(jnp.bfloat16) for p in pieces(rotation_t))
+    basis_out[...] = (
+        lax.dot_general(basis, high, across, preferred_element_type=jnp.float32)
+        + (lax.dot_general(basis, middle, across, preferred_element_type=jnp.float32)
+           + lax.dot_general(basis, low, across, preferred_element_type=jnp.float32))
+    ).astype(jnp.bfloat16)
+    curved_t = jnp.dot(rotation_t, G[...], precision=HIGHEST, preferred_element_type=jnp.float32)
+    squares = lax.dot_general(jnp.ones((8, K), jnp.float32), rotation_t * curved_t, across,
+                              precision=HIGHEST, preferred_element_type=jnp.float32)
+    sigma_out[...] = jnp.sqrt(squares[0:1])
+
+
+def rotated(gram, prior, start, coeffs, basis, total_frames):
+    vmem = pl.BlockSpec(memory_space=pltpu.VMEM)
+    return pl.pallas_call(
+        functools.partial(rotate_kernel, total_frames),
+        out_shape=(jax.ShapeDtypeStruct(basis.shape, jnp.bfloat16),
+                   jax.ShapeDtypeStruct(coeffs.shape, jnp.float32),
+                   jax.ShapeDtypeStruct((1, K), jnp.float32)),
+        in_specs=[vmem] * 5,
+        out_specs=(vmem,) * 3,
+        scratch_shapes=[pltpu.VMEM((K, K), jnp.float32), pltpu.VMEM((K, K), jnp.float32),
+                        pltpu.VMEM((K, 2 * K), jnp.float32)],
+    )(gram, prior.reshape(1, K), start, coeffs, basis)
 
 
 def body(raw_frames, dark_frame, dead_mask, frame_group, prior_sigma, start_rotation, basis):
@@ -66,21 +245,11 @@
         lax.all_gather(basis, "frames", axis=0, tiled=True),
         preferred_element_type=jnp.float32,
     )
-    coeffs = lax.psum(partial_value, "strips")
-    total_frames = frame_count * lax.axis_size("frames")
-    local_gram = jnp.dot(coeffs.T, coeffs, precision=lax.Precision.HIGHEST)
-    summed_gram = lax.psum(local_gram, "frames")
-    gram = jnp.diag(prior_sigma * prior_sigma) + summed_gram / total_frames
-    rotation = start_rotation
-    for step in range(ITERS):
-        rotation = orthonormalize(jnp.dot(gram, rotation, precision=lax.Precision.HIGHEST))
-    new_coeffs = jnp.dot(coeffs, rotation, precision=lax.Precision.HIGHEST)
-    new_basis = jnp.dot(
-        basis.astype(jnp.float32), rotation, precision=lax.Precision.HIGHEST
-    ).astype(jnp.bfloat16)
-    curved = jnp.dot(gram, rotation, precision=lax.Precision.HIGHEST)
-    new_sigma = jnp.sqrt(jnp.sum(rotation * curved, axis=0))
-    return (new_basis, new_coeffs, new_sigma)
+    frames, strips = lax.axis_size("frames"), lax.axis_size("strips")
+    coeffs, summed_gram = reduced(partial_value, frames // Y, strips)
+    new_basis, new_coeffs, new_sigma = rotated(
+        summed_gram, prior_sigma, start_rotation, coeffs, basis, frame_count * frames)
+    return (new_basis, new_coeffs, new_sigma.reshape(K))
 
 
 def solution(mesh):

time: 563 us -> 246 us (0.44); the launches traced: 553 us -> 245 us
  waiting for transfers between devices: 371 us -> 129 us
  other arithmetic: 102 us -> 9.81 us
  Pallas kernels: 0 us -> 66.1 us
  blocking collectives: 28.5 us -> 0 us
  matrix products: 20.9 us -> 11.6 us
    psum x1 -> x0, waiting for transfers between devices: 243 us -> none  [body(): summed_gram = lax.psum(local_gram, 'frames')]
    another operation x20 -> x0, other arithmetic: 91.8 us -> none  [the longest x12 49.6 us: orthonormalize(): factor = jnp.linalg.cholesky(normal)]
    pallas_call x0 -> x2, Pallas kernels: none -> 66.1 us  [the longest x1 38.3 us: reduced(): pl.pallas_call(functools.partial(reduce_kernel, Z, S), out_shape=(jax.Sha...]
    psum x1 -> x0, blocking collectives: 28.5 us -> none  [body(): coeffs = lax.psum(partial_value, 'strips')]
    dot_general x12 -> x0, matrix products: 8.81 us -> none  [the longest x4 4.52 us: body(): jnp.dot(gram, rotation, precision=lax.Precision.HIGHEST)]
  transfers between devices with their start and end apart: 4 -> 3, of which waited for: 4 -> 3; matrix products, arithmetic and copies ran while one was open for 3% -> 8% of each run, Pallas kernels for 0% -> 0%
where the time goes in v1:
time: 246 us; the launch traced here: 245 us
  waiting for transfers between devices  129 us (52%)
  Pallas kernels  66.1 us (27%)
  between operations  14.1 us (6%)
  matrix products  11.6 us (5%)
  starting transfers between devices  10.1 us (4%)
  other arithmetic  9.81 us (4%)
  local copies, waits for them, and re-layouts  4.76 us (2%)
    all_gather x1, waiting for transfers between devices, body(): lax.all_gather(basis, 'frames', axis=0, tiled=True)  123 us
    pallas_call x1, Pallas kernels, reduced(): pl.pallas_call(functools.partial(reduce_kernel, Z, S), out_shape=(jax.Sha...  38.3 us
    pallas_call x1, Pallas kernels, rotated(): pl.pallas_call(functools.partial(rotate_kernel, total_frames), out_shape=...  27.8 us
    convert_element_type x1, other arithmetic, body(): weighted = (frame_weight[:, None, None] * row_blur).astype(jnp.bfloat16)....  8.89 us
    dot_general x1, matrix products, body(): jnp.dot(weighted, lax.all_gather(basis, 'frames', axis=0, tiled=True), pr...  6.85 us
    ppermute x1, starting transfers between devices, extended(): after = lax.ppermute(first, axis, down)  5.6 us
  transfers between devices with their start and end apart: 3, of which 3 were waited for; matrix products, arithmetic and copies ran while one was open for 8% of the time, Pallas kernels for 0%

profile of v1, /device:TPU:1, one launch (start us, length us, event | category | flops | bytes accessed | tf_op | source)
XLA Modules:
  0.0 245.3 jit_solution(6903020991923679214)
XLA Ops:
  7.2 0.0 all-gather.2.cloned.1.call-start
  7.2 0.7 all-gather.2.cloned.1.call-update
  7.9 0.9 subtract_convert_fusion
  8.8 0.0 copy-start
  8.8 4.7 %fusion.18 = f32[64,64,512]{2,1,0:T(8,128)S(1)} fusion(bf16[64,64,512]{2,1,0:T(8,128)(2,1)} %param.7, f32[64,512]{1,0:T(8,128)S(1)} %subtract_convert_fusion, f32[64,512]{1,0:T(8,128)} %param.8), kind=kOutput, calls=%fused_computation.29 | convolution fusion | flops 2161639424 | bytes 12845056 | tf_op jit(solution)/shard_map/dot_general | solution.py:225
  13.6 0.2 fusion.54
  13.8 4.5 %collective-permute-start = (f32[64,3,512]{2,1,0:T(4,128)S(1)}, f32[64,3,512]{2,1,0:T(4,128)S(1)}, u32[]{:S(2)}, u32[]{:S(2)}) collective-permute-start(f32[64,3,512]{2,1,0:T(4,128)S(1)} %get-tuple-element.13), channel_id=1, source_target_pairs={{0,1},{1,2},{2,3},{3,4},{4,5},{5,6},{6,7},{8,9},{9,10},{10,11},{11... | collective-permute-start | bytes 1179656 | tf_op jit(solution)/shard_map/ppermute | solution.py:28
  18.4 5.6 %collective-permute-start.1 = (f32[64,3,512]{2,1,0:T(4,128)S(1)}, f32[64,3,512]{2,1,0:T(4,128)S(1)}, u32[]{:S(2)}, u32[]{:S(2)}) collective-permute-start(f32[64,3,512]{2,1,0:T(4,128)S(1)} %get-tuple-element.14), channel_id=1, source_target_pairs={{1,0},{2,1},{3,2},{4,3},{5,4},{6,5},{7,6},{9,8},{10,9},{11,10},{12... | collective-permute-start | bytes 1179656 | tf_op jit(solution)/shard_map/ppermute | solution.py:29
  24.0 0.0 copy-done
  24.0 0.5 collective-permute-done
  24.5 4.4 %collective-permute-done.1 = f32[64,3,512]{2,1,0:T(4,128)S(1)} collective-permute-done((f32[64,3,512]{2,1,0:T(4,128)S(1)}, f32[64,3,512]{2,1,0:T(4,128)S(1)}, u32[]{:S(2)}, u32[]{:S(2)}) %collective-permute-start.1) | collective-permute-done | bytes 393248 | tf_op jit(solution)/shard_map/ppermute | solution.py:29
  28.9 8.9 %fusion.5 = bf16[64,64,512]{2,1,0:T(8,128)(2,1)S(1)} fusion(f32[64,64,512]{2,1,0:T(8,128)S(1)} %fusion.18, f32[64,3,512]{2,1,0:T(4,128)S(1)} %collective-permute-done.1, f32[64,3,512]{2,1,0:T(4,128)S(1)} %collective-permute-done, f32[64]{0:T(128)S(1)} %convert_power_fusion), kind=kLoop, calls=%fused_computation.13 | loop fusion | flops 44040192 | bytes 13369600 | tf_op jit(solution)/shard_map/convert_element_type | solution.py:240
  37.7 4.5 %copy.10 = bf16[8,8,64,512]{3,1,2,0:T(8,128)(2,1)} copy(bf16[8,8,64,512]{3,2,1,0:T(8,128)(2,1)S(1)} %bitcast.10) | data formatting | bytes 8388608
  42.3 123.3 %all-gather.2.cloned.1.call-done = bf16[32768,128]{1,0:T(8,128)(2,1)} async-done(((bf16[512,128]{1,0:T(8,128)(2,1)}), bf16[32768,128]{1,0:T(8,128)(2,1)}) %all-gather.2.cloned.1.call-update) | async-done | bytes 8388624 | tf_op jit(solution)/shard_map/all_gather | solution.py:245
  165.5 6.9 %fusion.55.part_ref = f32[64,128]{1,0:T(8,128)} fusion(bf16[64,32768]{1,0:T(8,128)(2,1)} %bitcast.9, bf16[32768,128]{1,0:T(8,128)(2,1)} %all-gather.2.cloned.1.call-done), kind=kOutput, calls=%fused_computation.69 | convolution fusion | flops 536870912 | bytes 12615680 | tf_op jit(solution)/shard_map/dot_general | solution.py:243
  172.4 38.3 %shard_map.94 = (f32[64,128]{1,0:T(8,128)}, f32[128,128]{1,0:T(8,128)}) custom-call(f32[64,128]{1,0:T(8,128)} %fusion.55.part_ref), custom_call_target="tpu_custom_call" | custom-call | tf_op jit(solution)/shard_map/pallas_call | solution.py:112
  210.7 27.8 %shard_map.95 = (bf16[512,128]{1,0:T(8,128)(2,1)}, f32[64,128]{1,0:T(8,128)}, f32[1,128]{1,0:T(1,128)}) custom-call(f32[128,128]{1,0:T(8,128)} %get-tuple-element.8.gram_ref, f32[1,128]{1,0:T(1,128)} %bitcast.11, f32[128,128]{1,0:T(8,128)} %start_ref.1, f32[64,128]{1,0:T(8,128)} %get-tuple-element.9.coeffs_ref, bf16[512,128]{1,0:T(8,128)(2,1)} %basis_ref.1), custom_call_target="tpu_custom_call" | custom-call | tf_op jit(solution)/shard_map/pallas_call | solution.py:202
  (1 shorter events, 0.0 us)
Async XLA Ops:
  7.2 158.4 %all-gather.2.cloned.1.call-start = ((), (), s32[]{:S(2)}) async-start(), calls=%async_computation | async-start | bytes 8519680 | tf_op jit(solution)/shard_map/all_gather | solution.py:245
  8.8 15.1 %copy-start = (s32[64]{0:T(128)S(1)}, s32[64]{0:T(128)}, u32[]{:S(2)}) copy-start(s32[64]{0:T(128)} %param.10) | copy-start | bytes 772
  13.8 10.6 %collective-permute-start = (f32[64,3,512]{2,1,0:T(4,128)S(1)}, f32[64,3,512]{2,1,0:T(4,128)S(1)}, u32[]{:S(2)}, u32[]{:S(2)}) collective-permute-start(f32[64,3,512]{2,1,0:T(4,128)S(1)} %get-tuple-element.13), channel_id=1, source_target_pairs={{0,1},{1,2},{2,3},{3,4},{4,5},{5,6},{6,7},{8,9},{9,10},{10,11},{11... | collective-permute-start | bytes 1179656 | tf_op jit(solution)/shard_map/ppermute | solution.py:28
  18.4 10.5 %collective-permute-start.1 = (f32[64,3,512]{2,1,0:T(4,128)S(1)}, f32[64,3,512]{2,1,0:T(4,128)S(1)}, u32[]{:S(2)}, u32[]{:S(2)}) collective-permute-start(f32[64,3,512]{2,1,0:T(4,128)S(1)} %get-tuple-element.14), channel_id=1, source_target_pairs={{1,0},{2,1},{3,2},{4,3},{5,4},{6,5},{7,6},{9,8},{10,9},{11,10},{12... | collective-permute-start | bytes 1179656 | tf_op jit(solution)/shard_map/ppermute | solution.py:29
Sparse Core Ops, SparseCore 0:
  10.9 154.5 all-gather.1

commit v2 on v1

--- a/solution.py
+++ b/solution.py
@@ -11,6 +11,7 @@
 ITERS = 4
 K = 128
 Y = 4
+SPLIT = 192
 
 BLUR_TAPS = (1.0 / 64, 6.0 / 64, 15.0 / 64, 20.0 / 64, 15.0 / 64, 6.0 / 64, 1.0 / 64)
 DECAY_RATE = 0.7
@@ -18,36 +19,65 @@
 HIGHEST = lax.Precision.HIGHEST
 
 
-def extended(shard, sides, width):
-    for axis, dim in sides:
-        size, length = (lax.axis_size(axis), shard.shape[dim])
-        up = [(i, (i + 1) % size) for i in range(size - 1)]
-        down = [(j, i) for i, j in up]
-        last = lax.slice_in_dim(shard, length - width, length, axis=dim)
-        first = lax.slice_in_dim(shard, 0, width, axis=dim)
-        before = lax.ppermute(last, axis, up)
-        after = lax.ppermute(first, axis, down)
-        shard = jnp.concatenate([before, shard, after], axis=dim)
-    return shard
-
-
-def reduce_kernel(Z, S, part_ref, coeffs_ref, gram_ref,
+def window_kernel(Z, S, corrected_ref, weight_ref, basis_ref, coeffs_ref, gram_ref,
+                  full_basis, halo, blurred, weighted, part,
                   parts, local, ybuf, zbuf, full,
+                  own_sem, halo_send, halo_recv, ay_send, az_send, bz_send, by_send,
+                  a_recv, a_recv2, b_recv, b_recv2, bz_recv2,
                   s1, r1, s2, r2, s3, r3, s4, r4):
     f, s = lax.axis_index("frames"), lax.axis_index("strips")
     z, y = f // Y, f % Y
+    R, D, W = corrected_ref.shape
     NB = 2 * S
     rows = K // NB
+    f_cross = z * Y + (y + 2) % Y
     strip_peers = [(f, (s + d) % S) for d in range(1, S)]
     y_peers = [(z * Y + (y + d) % Y, s) for d in range(1, Y)]
     z_peers = [(((z + d) % Z) * Y + y, s) for d in range(1, Z)]
-    f_cross = z * Y + (y + 2) % Y
     cross_peers = [(f_cross, (s + d) % S) for d in range(1, S)]
+    everyone = strip_peers + y_peers + z_peers + cross_peers
+    z_up, z_down, y_up, y_down = z_peers[0], z_peers[-1], y_peers[0], y_peers[-1]
+    strip_up, strip_down = strip_peers[0], strip_peers[-1]
+
     barrier = pltpu.get_barrier_semaphore()
-    everyone = strip_peers + y_peers + z_peers + cross_peers
     for peer in everyone:
         pl.semaphore_signal(barrier, inc=1, device_id=peer, device_id_type=MESH)
-    pl.semaphore_wait(barrier, len(everyone))
+    own = pltpu.make_async_copy(basis_ref, full_basis.at[f], own_sem)
+    own.start()
+
+    offset = (lax.broadcasted_iota(jnp.int32, (W, W), 1)
+              - lax.broadcasted_iota(jnp.int32, (W, W), 0))
+    banded = jnp.zeros((W, W), jnp.float32)
+    for e in range(-3, 4):
+        banded = jnp.where(offset == e, BLUR_TAPS[e + 3], banded)
+    banded = banded.astype(jnp.bfloat16)
+    weight = jnp.broadcast_to(weight_ref[...], (D, W))
+
+    def column_blur(start, count):
+        def one(i, carry):
+            r = start + i
+            blurred[r + 3] = jnp.dot(corrected_ref[r], banded,
+                                     preferred_element_type=jnp.float32)
+            return carry
+        lax.fori_loop(0, count, one, 0)
+
+    def halo_blur():
+        for side in range(2):
+            arrived(halo.at[side], halo_recv.at[side])
+            inside = s > 0 if side == 0 else s < S - 1
+            for i in range(3):
+                value = jnp.dot(halo[side, i], banded, preferred_element_type=jnp.float32)
+                blurred[i if side == 0 else R + 3 + i] = jnp.where(inside, value, 0.0)
+
+    def row_blur(start, count):
+        def one(i, carry):
+            r = start + i
+            value = BLUR_TAPS[0] * blurred[r]
+            for e in range(1, 7):
+                value = value + BLUR_TAPS[e] * blurred[r + e]
+            weighted[r] = (weight * value).astype(jnp.bfloat16)
+            return carry
+        lax.fori_loop(0, count, one, 0)
 
     def send(src, dst, ssem, rsem, peer):
         copy = pltpu.make_async_remote_copy(
@@ -59,9 +89,119 @@
     def arrived(ref, sem):
         pltpu.make_async_copy(ref, ref, sem).wait()
 
-    sent = [send(part_ref, parts.at[s], s1.at[d], r1.at[s], peer)
-            for d, peer in enumerate(strip_peers)]
-    parts[s] = part_ref[...]
+    column_blur(0, R // 4)
+    tasks = [functools.partial(column_blur, q * (R // 4), R // 4) for q in range(1, 4)]
+    tasks.append(halo_blur)
+    tasks += [functools.partial(row_blur, q * (R // 4), R // 4) for q in range(4)]
+    own.wait()
+    pl.semaphore_wait(barrier, len(everyone))
+
+    cut = SPLIT
+    rest = W - cut
+    half = Z // 2
+
+    def a(slot, lo=0, hi=cut):
+        return full_basis.at[slot, pl.ds(lo, hi - lo)]
+
+    def b(slot, lo=0, hi=rest):
+        return full_basis.at[slot, pl.ds(cut + lo, hi - lo)]
+
+    def pass_on(ref, ssem, rsem, peer):
+        send(ref, ref, ssem.at[0], rsem, peer)
+
+    pass_on(b(f), bz_send, b_recv.at[f], z_up)
+    pass_on(b(f), bz_send, b_recv.at[f], z_down)
+    for peer in y_peers:
+        pass_on(a(f), ay_send, a_recv.at[f], peer)
+    pass_on(a(f), az_send, a_recv.at[f], z_up)
+    pass_on(a(f), az_send, a_recv.at[f], z_down)
+    pass_on(b(f), by_send, b_recv.at[f], y_up)
+    pass_on(b(f), by_send, b_recv.at[f], y_down)
+    sent = [send(corrected_ref.at[pl.ds(R - 3, 3)], halo.at[0], halo_send.at[0],
+                 halo_recv.at[0], strip_up),
+            send(corrected_ref.at[pl.ds(0, 3)], halo.at[1], halo_send.at[1],
+                 halo_recv.at[1], strip_down)]
+    for d in range(1, Y):
+        slot = z * Y + (y + d) % Y
+        arrived(a(slot), a_recv.at[slot])
+        pass_on(a(slot), az_send, a_recv.at[slot], z_up)
+        pass_on(a(slot), az_send, a_recv.at[slot], z_down)
+
+    def across_y(zz):
+        below, above = zz * Y + (y + Y - 1) % Y, zz * Y + (y + 1) % Y
+        arrived(b(below), b_recv.at[below])
+        pass_on(b(below, 0, rest // 2), by_send, b_recv.at[below], y_up)
+        arrived(b(above), b_recv.at[above])
+        pass_on(b(above, rest // 2, rest), by_send, b_recv2.at[zz], y_down)
+
+    for k in range(1, half):
+        lower, upper = (z + Z - k) % Z, (z + k) % Z
+        last = k == half - 1
+        for zz, peer, side in ((lower, z_up, 0), (upper, z_down, 1)):
+            slot = zz * Y + y
+            arrived(b(slot), b_recv.at[slot])
+            if not last:
+                pass_on(b(slot), bz_send, b_recv.at[slot], peer)
+            elif side == 0:
+                pass_on(b(slot, 0, rest // 2), bz_send, b_recv.at[slot], peer)
+            else:
+                pass_on(b(slot, rest // 2, rest), bz_send, bz_recv2.at[0], peer)
+            pass_on(b(slot), by_send, b_recv.at[slot], y_up)
+            pass_on(b(slot), by_send, b_recv.at[slot], y_down)
+        for c in range(Y):
+            for zz, peer, side in ((lower, z_up, 0), (upper, z_down, 1)):
+                slot = zz * Y + c
+                arrived(a(slot), a_recv.at[slot])
+                if not last:
+                    pass_on(a(slot), az_send, a_recv.at[slot], peer)
+                elif side == 0:
+                    pass_on(a(slot, 0, cut // 2), az_send, a_recv.at[slot], peer)
+                else:
+                    pass_on(a(slot, cut // 2, cut), az_send, a_recv2.at[c], peer)
+        if k == 1:
+            across_y(z)
+        else:
+            across_y((z + Z - k + 1) % Z)
+            across_y((z + k - 1) % Z)
+        share = -(-len(tasks) // (half - k + 1))
+        for task in tasks[:share]:
+            task()
+        tasks = tasks[share:]
+    far = (z + half) % Z
+    slot = far * Y + y
+    arrived(b(slot, 0, rest // 2), b_recv.at[slot])
+    arrived(b(slot, rest // 2, rest), bz_recv2.at[0])
+    pass_on(b(slot), by_send, b_recv.at[slot], y_up)
+    pass_on(b(slot), by_send, b_recv.at[slot], y_down)
+    across_y((z + Z - half + 1) % Z)
+    if half > 2:
+        across_y((z + half - 1) % Z)
+    else:
+        across_y((z + 1) % Z)
+    for task in tasks:
+        task()
+    for c in range(Y):
+        slot = far * Y + c
+        arrived(a(slot, 0, cut // 2), a_recv.at[slot])
+        arrived(a(slot, cut // 2, cut), a_recv2.at[c])
+    across_y(far)
+    for d in range(Z):
+        zz = (z + d) % Z
+        slot = zz * Y + (y + 2) % Y
+        arrived(b(slot, 0, rest // 2), b_recv.at[slot])
+        arrived(b(slot, rest // 2, rest), b_recv2.at[zz])
+
+    def project(i, total):
+        for r in range(4):
+            total = total + jnp.dot(weighted[4 * i + r], full_basis[4 * i + r],
+                                    preferred_element_type=jnp.float32)
+        return total
+
+    part[...] = lax.fori_loop(0, R // 4, project, jnp.zeros((D, K), jnp.float32))
+
+    sent += [send(part, parts.at[s], s1.at[d], r1.at[s], peer)
+             for d, peer in enumerate(strip_peers)]
+    parts[s] = part[...]
     for d in range(1, S):
         other = (s + d) % S
         arrived(parts.at[other], r1.at[other])
@@ -100,32 +240,44 @@
         other = (mine + d) % NB
         arrived(full.at[other], r4.at[other])
     gram_ref[...] = full[...].reshape(K, K)
+
     for copy in sent:
         copy.wait_send()
-
-
-def reduced(part, Z, S):
-    frames = part.shape[0]
+    arrived(full_basis.at[pl.ds(0, Y - 1), pl.ds(0, cut)], ay_send.at[0])
+    arrived(full_basis.at[pl.ds(0, Y * (Z - 1)), pl.ds(0, cut)], az_send.at[0])
+    arrived(full_basis.at[pl.ds(0, Z - 1), pl.ds(cut, rest)], bz_send.at[0])
+    arrived(full_basis.at[pl.ds(0, 3 * Z), pl.ds(cut, rest)], by_send.at[0])
+
+
+def windowed(corrected, weight, basis, Z, S):
+    R, D, W = corrected.shape
     rows = K // (2 * S)
     dma = pltpu.SemaphoreType.DMA
     vmem = pl.BlockSpec(memory_space=pltpu.VMEM)
+    f32, bf16 = jnp.float32, jnp.bfloat16
     return pl.pallas_call(
-        functools.partial(reduce_kernel, Z, S),
-        out_shape=(jax.ShapeDtypeStruct((frames, K), jnp.float32),
-                   jax.ShapeDtypeStruct((K, K), jnp.float32)),
-        in_specs=[vmem],
+        functools.partial(window_kernel, Z, S),
+        out_shape=(jax.ShapeDtypeStruct((D, K), f32), jax.ShapeDtypeStruct((K, K), f32)),
+        in_specs=[vmem] * 3,
         out_specs=(vmem, vmem),
         scratch_shapes=[
-            pltpu.VMEM((S, frames, K), jnp.float32),
-            pltpu.VMEM((2 * S, rows, K), jnp.float32),
-            pltpu.VMEM((Y, rows, K), jnp.float32),
-            pltpu.VMEM((Z, rows, K), jnp.float32),
-            pltpu.VMEM((2 * S, rows, K), jnp.float32),
+            pltpu.VMEM((Z * Y, W, K), bf16),
+            pltpu.VMEM((2, 3, D, W), bf16),
+            pltpu.VMEM((R + 6, D, W), f32),
+            pltpu.VMEM((R, D, W), bf16),
+            pltpu.VMEM((D, K), f32),
+            pltpu.VMEM((S, D, K), f32),
+            pltpu.VMEM((2 * S, rows, K), f32),
+            pltpu.VMEM((Y, rows, K), f32),
+            pltpu.VMEM((Z, rows, K), f32),
+            pltpu.VMEM((2 * S, rows, K), f32),
+            dma, dma((2,)), dma((2,)), dma((1,)), dma((1,)), dma((1,)), dma((1,)),
+            dma((Z * Y,)), dma((Y,)), dma((Z * Y,)), dma((Z,)), dma((1,)),
             dma((S,)), dma((S,)), dma((Y,)), dma((Y,)),
             dma((Z,)), dma((Z,)), dma((2 * S,)), dma((2 * S,)),
         ],
         compiler_params=pltpu.CompilerParams(collective_id=0, has_side_effects=True),
-    )(part)
+    )(corrected, weight, basis)
 
 
 def pieces(x):
@@ -216,37 +368,12 @@
     corrected = (
         (raw_frames.astype(jnp.float32) - dark_frame) * (1 - dead_mask).astype(jnp.float32)
     ).astype(jnp.bfloat16)
-    position = jnp.arange(columns)
-    offsets = position[None, :] - position[:, None]
-    banded = jnp.zeros((columns, columns), jnp.float32)
-    for shift_by in range(-3, 4):
-        banded = banded + jnp.where(offsets == shift_by, BLUR_TAPS[shift_by + 3], 0.0)
-    banded = banded.astype(jnp.bfloat16)
-    column_blur = jnp.dot(
-        corrected.reshape(frame_count * strip_rows, columns),
-        banded,
-        preferred_element_type=jnp.float32,
-    )
-    column_blur = column_blur.reshape(frame_count, strip_rows, columns)
-    padded = extended(column_blur, (("strips", 1),), 3)
-    row_blur = BLUR_TAPS[0] * padded[:, 0:strip_rows, :]
-    for offset in range(1, 7):
-        row_blur = row_blur + BLUR_TAPS[offset] * padded[:, offset : offset + strip_rows, :]
     frame_weight = jnp.power(
         jnp.float32(DECAY_RATE), (GROUPS - 1 - frame_group).astype(jnp.float32)
     )
-    weighted = (
-        (frame_weight[:, None, None] * row_blur)
-        .astype(jnp.bfloat16)
-        .reshape(frame_count, strip_rows * columns)
-    )
-    partial_value = jnp.dot(
-        weighted,
-        lax.all_gather(basis, "frames", axis=0, tiled=True),
-        preferred_element_type=jnp.float32,
-    )
     frames, strips = lax.axis_size("frames"), lax.axis_size("strips")
-    coeffs, summed_gram = reduced(partial_value, frames // Y, strips)
+    coeffs, summed_gram = windowed(
+        corrected.transpose(1, 0, 2), frame_weight[:, None], basis, frames // Y, strips)
     new_basis, new_coeffs, new_sigma = rotated(
         summed_gram, prior_sigma, start_rotation, coeffs, basis, frame_count * frames)
     return (new_basis, new_coeffs, new_sigma.reshape(K))

time: 246 us -> 139 us (0.57)
  waiting for transfers between devices: 129 us -> 0 us
  Pallas kernels: 66.1 us -> 129 us
  between operations: 14.1 us -> 0.65 us
  matrix products: 11.6 us -> 0 us
  starting transfers between devices: 10.1 us -> 0 us
  local copies, waits for them, and re-layouts: 4.76 us -> 0.72 us
    all_gather x1 -> x0, waiting for transfers between devices: 123 us -> none  [body(): lax.all_gather(basis, 'frames', axis=0, tiled=True)]
    pallas_call x1, Pallas kernels: 38.3 us -> 101 us  [windowed(): pl.pallas_call(functools.partial(window_kernel, Z, S), out_shape=(jax.Sha...]
    dot_general x2 -> x0, matrix products: 11.6 us -> none  [the longest x1 6.85 us: body(): jnp.dot(weighted, lax.all_gather(basis, 'frames', axis=0, tiled=True), pr...]
    ppermute x2 -> x0, starting transfers between devices: 10.1 us -> none  [the longest x1 5.6 us: extended(): after = lax.ppermute(first, axis, down)]
    convert_element_type x1 -> x0, other arithmetic: 8.89 us -> none  [body(): weighted = (frame_weight[:, None, None] * row_blur).astype(jnp.bfloat16)....]
    transpose x0 -> x1, other arithmetic: none -> 7.51 us  [body(): corrected.transpose(1, 0, 2)]
    ppermute x2 -> x0, waiting for transfers between devices: 4.87 us -> none  [the longest x1 4.4 us: extended(): after = lax.ppermute(first, axis, down)]
    unnamed x3 -> x2, local copies, waits for them, and re-layouts: 4.51 us -> 0.01 us
  transfers between devices with their start and end apart: 3 -> 0, of which waited for: 3 -> 0; matrix products, arithmetic and copies ran while one was open for 8% -> 0% of each run, Pallas kernels for 0% -> 0%
where the time goes in v2:
time: 139 us; the launch traced here: 138 us
  Pallas kernels  129 us (93%)
  other arithmetic  8.43 us (6%)
    pallas_call x1, Pallas kernels, windowed(): pl.pallas_call(functools.partial(window_kernel, Z, S), out_shape=(jax.Sha...  101 us
    pallas_call x1, Pallas kernels, rotated(): pl.pallas_call(functools.partial(rotate_kernel, total_frames), out_shape=...  27.8 us
    transpose x1, other arithmetic, body(): corrected.transpose(1, 0, 2)  7.51 us

profile of v2, /device:TPU:1, one launch (start us, length us, event | category | flops | bytes accessed | tf_op | source)
XLA Modules:
  0.0 138.5 jit_solution(14122330179711294624)
XLA Ops:
  0.6 0.9 subtract_convert_fusion
  1.6 0.0 copy-start
  1.6 7.5 %fusion.corrected_ref = bf16[64,64,512]{2,1,0:T(8,128)(2,1)} fusion(bf16[64,64,512]{2,1,0:T(8,128)(2,1)} %param.7, f32[64,512]{1,0:T(8,128)S(1)} %subtract_convert_fusion, f32[64,512]{1,0:T(8,128)} %param.8), kind=kLoop, calls=%fused_computation.1 | loop fusion | flops 8388608 | bytes 8650752 | tf_op jit(solution)/shard_map/transpose | solution.py:376
  9.1 0.0 copy-done
  9.1 0.7 copy.11.weight_ref
  9.8 100.9 %shard_map.94 = (f32[64,128]{1,0:T(8,128)}, f32[128,128]{1,0:T(8,128)}) custom-call(bf16[64,64,512]{2,1,0:T(8,128)(2,1)} %fusion.corrected_ref, f32[64,1]{1,0:T(8,128)} %copy.11.weight_ref, bf16[512,128]{1,0:T(8,128)(2,1)} %basis_ref.3), custom_call_target="tpu_custom_call" | custom-call | tf_op jit(solution)/shard_map/pallas_call | solution.py:258
  110.7 27.8 %shard_map.95 = (bf16[512,128]{1,0:T(8,128)(2,1)}, f32[64,128]{1,0:T(8,128)}, f32[1,128]{1,0:T(1,128)}) custom-call(f32[128,128]{1,0:T(8,128)} %get-tuple-element.8.gram_ref, f32[1,128]{1,0:T(1,128)} %bitcast.6, f32[128,128]{1,0:T(8,128)} %start_ref.1, f32[64,128]{1,0:T(8,128)} %get-tuple-element.9.coeffs_ref, bf16[512,128]{1,0:T(8,128)(2,1)} %basis_ref.3), custom_call_target="tpu_custom_call" | custom-call | tf_op jit(solution)/shard_map/pallas_call | solution.py:354
  (1 shorter events, 0.0 us)
Async XLA Ops:
  1.6 7.5 %copy-start = (s32[64]{0:T(128)S(1)}, s32[64]{0:T(128)}, u32[]{:S(2)}) copy-start(s32[64]{0:T(128)} %param.10) | copy-start | bytes 772
